TPU v7x, 512 devices: a whole 4x4x16 slice. The times are simulated.
512 devices in a mesh: grid: 64 (over y, z), batch: 8 (over x, core).
Axes of the slice: x: 4, y: 4, z: 16, core: 2. Of those that a mesh axis runs over, the one named last changes fastest.
Arguments:
- inputs: bfloat16 [8, 256, 65536], P('batch', None, 'grid'), may hold values from -6 to 6
- cotangent: bfloat16 [8, 256, 65536], P('batch', None, 'grid'), may hold values from -8 to 8
- weights: bfloat16 [512, 8, 9216], P('grid', 'batch'), may hold values from -0.375 to 0.375
- gate_logits: float32 [8, 256, 2], replicated, may hold values from -5 to 5
- routes: int32 [8, 256, 2], replicated, may hold values from 0 to 511, as said below
Outputs:
- d_inputs: bfloat16 [8, 256, 65536], P('batch', None, 'grid')
- d_weights: float32 [512, 8, 9216], P('grid', 'batch')
- gate_grad: float32 [8, 256, 2], P(None, 'grid')
Inputs may be any that keep to these rules, and one draw needn't show every extreme that they name: Expert e is owned by grid index e // 8. The 64 routes of the patches g * 4 to (g + 1) * 4 - 1 of all samples name experts of one owner at most 1 times, for every grid index g; in every draw some owner is named exactly 1 times by the routes of every grid index. The 2 routes of a patch name different experts.
All inputs are finite; a program needn't handle non-finite values.
Results may differ from a plain program's by a relative error of at most 0.0051.
Values may be sent and summed in bfloat16 or wider, within the bound.
A program may use at most 128 MiB of HBM per device.

v0:
```python
import functools

import jax
import jax.numpy as jnp
from jax import lax
from jax.experimental import pallas as pl
from jax.experimental.pallas import tpu as pltpu
from jax.sharding import PartitionSpec as P

MESH = pl.DeviceIdType.MESH
CG = 32
SIDE = 16
PIX = SIDE * SIDE
TAPS = 9
EXP = 8
TOP = 2
NSUB = 4
ES = EXP // NSUB
UR = 80
BF = jnp.bfloat16
F32 = jnp.float32
Z_SIZE = 16


def step_kernel(
    ny, nz, nb, pcol,
    x_hbm, dy_hbm, w_ref, tab_ref, rows_ref, gate_ref, gatev_ref,
    dx_hbm, dw_hbm, gg_ref,
    xg, dyg, taps_buf, wg, ws, wr, gb, gs, gr, rr, rs, dxs, parts, dots_s, dots_r, dw_v,
    tap_mask, tail_mask, tail_mask_bf, block,
    act_send, act_recv, act_loc, ag_send, ag_recv, wy_send, wy_recv, gy_send, gy_recv,
    rs_send, rs_recv, dx_send, dx_recv, dot_send, dot_recv, out_sem,
):
    half = nz // 2
    nx = nb // 2
    patches = nb * pcol
    ticks = half * NSUB
    grid_id = lax.axis_index("grid")
    b = lax.axis_index("batch")
    y = lax.div(grid_id, nz)
    z = lax.rem(grid_id, nz)
    xi = lax.div(b, 2)
    core = lax.rem(b, 2)
    right = y * nz + lax.rem(z + 1, nz)
    left = y * nz + lax.rem(z + nz - 1, nz)
    hop_to = (right, left)

    def split(j):
        q = lax.div(j, 2)
        far = q + lax.div(q, 2) * (1 - 2 * lax.rem(q, 2))
        return far, lax.rem(j, 2)

    def sender_of(j):
        far, other = split(j)
        return lax.rem(xi + nx - far, nx) * 2 + lax.rem(core + other, 2)

    def receiver_of(j):
        far, other = split(j)
        return lax.rem(xi + far, nx) * 2 + lax.rem(core + other, 2)

    def tile_at(d):
        return lax.rem(y + d, ny)

    barrier = pltpu.get_barrier_semaphore()
    peers = [(right, b), (left, b)]
    peers += [(tile_at(d) * nz + z, b) for d in range(1, ny)]
    peers += [(grid_id, receiver_of(jnp.int32(j))) for j in range(1, nb)]
    for peer in peers:
        pl.semaphore_signal(barrier, inc=1, device_id=peer, device_id_type=MESH)
    pl.semaphore_wait(barrier, len(peers))

    def act_copy(which, j):
        src, dst = ((dy_hbm, dyg), (x_hbm, xg))[which]
        peer = receiver_of(j)
        return pltpu.make_async_remote_copy(
            src_ref=src.at[0, pl.ds(pl.multiple_of(peer * CG, CG), CG), :],
            dst_ref=dst.at[b],
            send_sem=act_send.at[which, j],
            recv_sem=act_recv.at[which, j],
            device_id=(grid_id, peer),
            device_id_type=MESH,
        )

    def act_local(which):
        src, dst = ((dy_hbm, dyg), (x_hbm, xg))[which]
        return pltpu.make_async_copy(
            src.at[0, pl.ds(pl.multiple_of(b * CG, CG), CG), :], dst.at[b], act_loc.at[which]
        )

    def ag_copy(way, s, c, first):
        origin = lax.rem(z + nz - (s - 1), nz) if way == 0 else lax.rem(z + (s - 1), nz)
        piece = pl.ds(c * ES, ES)
        return pltpu.make_async_remote_copy(
            src_ref=w_ref.at[piece] if first else wg.at[origin, piece],
            dst_ref=wg.at[origin, piece],
            send_sem=ag_send.at[way, s - 1, c],
            recv_sem=ag_recv.at[way, s - 1, c],
            device_id=(hop_to[way], b),
            device_id_type=MESH,
        )

    def wy_copy(d, rel):
        zo = lax.rem(z + rel, nz)
        return pltpu.make_async_remote_copy(
            src_ref=ws.at[d - 1, rel],
            dst_ref=wr.at[y, zo],
            send_sem=wy_send.at[d - 1, rel],
            recv_sem=wy_recv.at[d - 1, rel],
            device_id=(tile_at(d) * nz + z, b),
            device_id_type=MESH,
        )

    def gy_copy(d, rel):
        return pltpu.make_async_remote_copy(
            src_ref=gs.at[d - 1, rel],
            dst_ref=gr.at[d, rel],
            send_sem=gy_send.at[d - 1, rel],
            recv_sem=gy_recv.at[d - 1, rel],
            device_id=(tile_at(d) * nz + z, b),
            device_id_type=MESH,
        )

    def rs_copy(way, t, c):
        return pltpu.make_async_remote_copy(
            src_ref=rs.at[way, t, c],
            dst_ref=rr.at[way, t, c],
            send_sem=rs_send.at[way, t, c],
            recv_sem=rs_recv.at[way, t, c],
            device_id=(hop_to[way], b),
            device_id_type=MESH,
        )

    def dx_copy(j):
        s = sender_of(j)
        return pltpu.make_async_remote_copy(
            src_ref=dxs.at[s],
            dst_ref=dx_hbm.at[0, pl.ds(pl.multiple_of(b * CG, CG), CG), :],
            send_sem=dx_send.at[j],
            recv_sem=dx_recv.at[j],
            device_id=(grid_id, s),
            device_id_type=MESH,
        )

    def dot_copy(j):
        return pltpu.make_async_remote_copy(
            src_ref=dots_s,
            dst_ref=dots_r.at[j],
            send_sem=dot_send.at[j],
            recv_sem=dot_recv.at[j],
            device_id=(grid_id, receiver_of(j)),
            device_id_type=MESH,
        )

    act_local(0).start()
    act_local(1).start()
    for way in (0, 1):
        for c in range(NSUB):
            if half > 1 or (c < NSUB // 2) == (way == 0):
                ag_copy(way, 1, c, True).start()
    for j in range(1, nb):
        act_copy(0, jnp.int32(j)).start()
        act_copy(1, jnp.int32(j)).start()

    lane = lax.broadcasted_iota(jnp.int32, (8, PIX), 1)
    column = lax.rem(lane, SIDE)
    row = lax.div(lane, SIDE)
    for t in range(TAPS):
        down, over = t // 3 - 1, t % 3 - 1
        inside = (row - down >= 0) & (row - down < SIDE) & (column - over >= 0) & (column - over < SIDE)
        tap_mask[t] = jnp.where(inside, 1.0, 0.0).astype(F32)
    tail_row = lax.div(lax.broadcasted_iota(jnp.int32, (CG, 128), 0), 16)
    tail_lane = lax.div(lax.broadcasted_iota(jnp.int32, (CG, 128), 1), CG)
    tail = jnp.where(tail_row == tail_lane, 1.0, 0.0).astype(F32)
    tail_mask[...] = tail
    tail_mask_bf[...] = tail.astype(BF)
    parts[...] = jnp.zeros_like(parts)
    for c in range(NSUB):
        rr[1 if c < NSUB // 2 else 0, 0, c] = jnp.zeros((ES, UR, 128), BF)

    def expert_of(tile, zo):
        return lax.rem(tab_ref[tile, y * nz + zo], EXP)

    def pick(rel):
        zo = lax.rem(z + rel, nz)
        block[...] = wg[zo]
        wr[y, zo] = block[expert_of(y, zo)]
        for d in range(1, ny):
            ws[d - 1, rel] = block[expert_of(tile_at(d), zo)]

    def send_picks(rel):
        for d in range(1, ny):
            wy_copy(d, rel).start()

    def patch_lanes(p):
        return pl.ds(pl.multiple_of(p * PIX, PIX), PIX)

    def grad_patch(j, p):
        s = sender_of(j)
        index = s * pcol + p
        dy = dyg[s, :, patch_lanes(p)].astype(F32).reshape(CG // 8, 8, PIX)
        for t in range(TAPS):
            shift = ((t // 3 - 1) * SIDE + (t % 3 - 1)) % PIX
            moved = dy if shift == 0 else pltpu.roll(dy, shift, 2) * tap_mask[t][None]
            moved = moved.reshape(CG, PIX).astype(BF)
            if t < TAPS - 1:
                taps_buf[index, t * CG : (t + 1) * CG, :] = moved
            else:
                for k in range(4):
                    taps_buf[index, (t + k) * CG : (t + k + 1) * CG, :] = moved
        xp = xg[s, :, patch_lanes(p)]
        dims = (((1,), (1,)), ((), ()))
        main = lax.dot_general(xp, taps_buf[index, : 8 * CG, :], dims, preferred_element_type=F32)
        last = lax.dot_general(xp, taps_buf[index, 8 * CG :, :], dims, preferred_element_type=F32)
        last = last * tail_mask[...]
        gb[index, 0:32, :] = main[:, :128]
        gb[index, 32:64, :] = main[:, 128:]
        gb[index, 64:80, :] = last[:16] + last[16:]

    def grad_stage(rel):
        zo = lax.rem(z + rel, nz)
        for d in range(ny):
            route = lax.div(tab_ref[y, tile_at(d) * nz + zo], EXP)
            value = (gb[lax.div(route, TOP)] * gate_ref[0, route]).astype(BF)
            if d == 0:
                gr[0, rel] = value
            else:
                gs[d - 1, rel] = value

    def route_unit(route):
        owner = lax.div(rows_ref[y, route], EXP)
        return wr[lax.div(owner, nz), lax.rem(owner, nz)]

    def dx_patch(j, p):
        s = sender_of(j)
        index = s * pcol + p
        mains, tails = [], []
        for k in range(TOP):
            unit = route_unit(index * TOP + k)
            mains.append(jnp.concatenate([unit[0:32], unit[32:64]], axis=1))
            tails.append(jnp.concatenate([unit[64:80], unit[64:80]], axis=0) * tail_mask_bf[...])
        adjoint = jnp.dot(
            jnp.concatenate(mains, axis=0), taps_buf[index, : 8 * CG, :], preferred_element_type=F32
        ) + jnp.dot(
            jnp.concatenate(tails, axis=0), taps_buf[index, 8 * CG :, :], preferred_element_type=F32
        )
        xp = xg[s, :, patch_lanes(p)].astype(F32)
        total = jnp.zeros((CG, PIX), F32)
        for k in range(TOP):
            one = adjoint[k * CG : (k + 1) * CG]
            prod = xp * one
            prod = (prod[0:8] + prod[8:16]) + (prod[16:24] + prod[24:32])
            prod = prod[:, :128] + prod[:, 128:]
            parts[pl.ds(index * TOP + k, 1), :] = jnp.sum(prod, axis=0, keepdims=True)
            total = total + (gate_ref[0, index * TOP + k] * one).astype(BF).astype(F32)
        dxs[s, :, patch_lanes(p)] = total.astype(BF)

    def own_part(rel, e):
        zo = lax.rem(z + rel, nz)
        total = None
        for d in range(ny):
            tile = lax.rem(y + ny - d, ny)
            hit = jnp.where(expert_of(tile, zo) == e, 1.0, 0.0).astype(F32)
            term = gr[d, rel].astype(F32) * hit
            total = term if total is None else total + term
        return total

    def rs_add(way, t, c, fresh):
        rel = half - t if way == 0 else nz - half + t
        for k in range(ES):
            value = own_part(rel, c * ES + k)
            if not fresh:
                value = value + rr[way, t - 1, c, k].astype(F32)
            rs[way, t, c, k] = value.astype(BF)

    def wait_grads(rel):
        for d in range(1, ny):
            gy_copy(d, rel).wait_recv()

    wg[z] = w_ref[...]
    pick(jnp.int32(0))

    def phase_one(k, carry):
        s = lax.div(k, NSUB) + 1
        c = lax.rem(k, NSUB)
        low = c < NSUB // 2
        for way in (0, 1):
            mine = low if way == 0 else jnp.logical_not(low)

            @pl.when(jnp.logical_or(s < half, mine))
            def _():
                ag_copy(way, s, c, False).wait_recv()

            @pl.when(jnp.logical_or(s + 1 < half, jnp.logical_and(s + 1 == half, mine)))
            def _():
                ag_copy(way, s + 1, c, False).start()

        @pl.when(c == 0)
        def _():
            send_picks(s - 1)

            @pl.when(s > 1)
            def _():
                send_picks(nz - s + 1)

        @pl.when(k < patches)
        def _():
            j = lax.div(k, pcol)

            @pl.when(lax.rem(k, pcol) == 0)
            def _():
                @pl.when(j == 0)
                def _():
                    act_local(0).wait()
                    act_local(1).wait()

                @pl.when(j > 0)
                def _():
                    act_copy(0, j).wait_recv()
                    act_copy(1, j).wait_recv()

            grad_patch(j, lax.rem(k, pcol))

        @pl.when(c == NSUB - 1)
        def _():
            pick(s)

            @pl.when(s < half)
            def _():
                pick(nz - s)

        return carry

    lax.fori_loop(0, ticks, phase_one, 0)

    def stage_one(i, carry):
        rel = lax.rem(half + lax.div(i + 1, 2) * (1 - 2 * lax.rem(i, 2)) + nz, nz)
        grad_stage(rel)
        return carry

    def stage_two(i, carry):
        rel = lax.rem(half + lax.div(i + 1, 2) * (1 - 2 * lax.rem(i, 2)) + nz, nz)
        for d in range(1, ny):
            gy_copy(d, rel).start()
        return carry

    send_picks(jnp.int32(half))
    lax.fori_loop(0, nz, stage_one, 0)
    lax.fori_loop(0, nz, stage_two, 0)

    def wait_kernels(rel, carry):
        for d in range(1, ny):
            wy_copy(d, rel).wait_recv()
        return carry

    lax.fori_loop(0, nz, wait_kernels, 0)

    wait_grads(jnp.int32(half))
    for c in range(NSUB):
        rs_add(0 if c < NSUB // 2 else 1, 0, c, True)

    def dx_tick(k):
        i = k - 1
        j = nb - 1 - lax.div(i, pcol)

        @pl.when(jnp.logical_and(i >= 0, i < patches))
        def _():
            dx_patch(j, lax.rem(i, pcol))

        return i

    def dx_flush(k):
        done = k - 2

        @pl.when(jnp.logical_and(done >= 0, jnp.logical_and(done < patches, lax.rem(done, pcol) == pcol - 1)))
        def _():
            j = nb - 1 - lax.div(done, pcol)

            @pl.when(j > 0)
            def _():
                dx_copy(j).start()

    dx_tick(jnp.int32(1))
    for c in range(NSUB):
        rs_copy(0 if c < NSUB // 2 else 1, 0, c).start()

    def phase_two(k, carry):
        t = lax.div(k, NSUB)
        c = lax.rem(k, NSUB)
        low = c < NSUB // 2

        @pl.when(c == 0)
        def _():
            wait_grads(half - t)
            wait_grads(nz - half + t)

        for way in (0, 1):
            mine = low if way == 0 else jnp.logical_not(low)

            @pl.when(jnp.logical_or(t > 1, mine))
            def _():
                rs_copy(way, t - 1, c).wait_recv()

            rs_add(way, t, c, False)
        dx_flush(k - NSUB + 2)
        dx_tick(k - NSUB + 2)
        for way in (0, 1):
            rs_copy(way, t, c).start()
        return carry

    lax.fori_loop(NSUB, ticks, phase_two, 0)
    tail_ticks = range(ticks - NSUB + 2, patches + 3)
    for k in tail_ticks:
        dx_flush(jnp.int32(k))
        dx_tick(jnp.int32(k))

    own_dx = pltpu.make_async_copy(
        dxs.at[b], dx_hbm.at[0, pl.ds(pl.multiple_of(b * CG, CG), CG), :], out_sem.at[0]
    )
    own_dx.start()
    dots = jnp.sum(parts[...].T, axis=0, keepdims=True).astype(BF).astype(F32)
    dots_s[...] = jnp.broadcast_to(dots, (8, 128))

    wait_grads(jnp.int32(0))
    last = half - 1
    for c in range(NSUB):
        for way in (0, 1):
            if half > 1 or (c < NSUB // 2) == (way == 0):
                rs_copy(way, last, c).wait_recv()
        if c == 0:
            for j in range(1, nb):
                dot_copy(jnp.int32(j)).start()
        for k in range(ES):
            value = own_part(jnp.int32(0), c * ES + k)
            value = value + rr[0, last, c, k].astype(F32) + rr[1, last, c, k].astype(F32)
            dw_v[c * ES + k] = value * (1.0 / SIDE)
    out_dw = pltpu.make_async_copy(dw_v, dw_hbm, out_sem.at[1])
    out_dw.start()

    total = dots_s[...]
    for j in range(1, nb):
        dot_copy(jnp.int32(j)).wait_recv()
        total = total + dots_r[j]
    gates = gatev_ref[...]
    gg_ref[...] = gates * (1.0 - gates) * total * (1.0 / SIDE)

    for j in range(1, nb):
        act_copy(0, jnp.int32(j)).wait_send()
        act_copy(1, jnp.int32(j)).wait_send()
        dot_copy(jnp.int32(j)).wait_send()
        dx_copy(jnp.int32(j)).wait_send()
        dx_copy(jnp.int32(j)).wait_recv()

    def drain_ring(k, carry):
        s = lax.div(k, NSUB)
        c = lax.rem(k, NSUB)
        low = c < NSUB // 2
        for way in (0, 1):
            mine = low if way == 0 else jnp.logical_not(low)

            @pl.when(jnp.logical_or(s + 1 < half, mine))
            def _():
                ag_copy(way, s + 1, c, False).wait_send()

            @pl.when(jnp.logical_or(s > 0, mine))
            def _():
                rs_copy(way, s, c).wait_send()

        return carry

    lax.fori_loop(0, ticks, drain_ring, 0)

    def drain_rows(rel, carry):
        for d in range(1, ny):
            wy_copy(d, rel).wait_send()
            gy_copy(d, rel).wait_send()
        return carry

    lax.fori_loop(0, nz, drain_rows, 0)
    own_dx.wait()
    out_dw.wait()


def per_device(nz, inputs, cotangent, weights, gate_logits, routes):
    grid_size = lax.axis_size("grid")
    nb = lax.axis_size("batch")
    ny = grid_size // nz
    half = nz // 2
    _, channels, width = inputs.shape
    pcol = width // PIX
    patches = nb * pcol
    count = patches * TOP
    index = lax.axis_index("grid")
    y, z = index // nz, index % nz

    kernels = weights.reshape(EXP, CG, CG, TAPS)
    main = kernels[..., :8].reshape(EXP, CG, CG, 2, 4).transpose(0, 3, 2, 4, 1).reshape(EXP, 64, 128)
    last = kernels[..., 8].reshape(EXP, CG, 2, 16).transpose(0, 3, 2, 1).reshape(EXP, 16, 64)
    units = jnp.concatenate([main, jnp.pad(last, ((0, 0), (0, 0), (0, 64)))], axis=1)

    near = routes.reshape(nb, ny, nz, pcol, TOP)
    near = lax.dynamic_index_in_dim(near, z, 2, keepdims=False)
    rows = near.transpose(1, 0, 2, 3).reshape(ny, count)
    code = jnp.arange(count, dtype=jnp.int32)[None, :] * EXP + rows % EXP
    named = (rows // EXP)[:, None, :] == jnp.arange(grid_size, dtype=jnp.int32)[None, :, None]
    table = jnp.sum(jnp.where(named, code[:, None, :], 0), axis=2)
    own = lax.dynamic_slice_in_dim(gate_logits, index * pcol, pcol, 1).reshape(1, count)
    gates = jax.nn.sigmoid(own)
    gates = jnp.pad(gates, ((0, 0), (0, 128 - count)))

    vmem, smem, hbm = (
        pl.BlockSpec(memory_space=pltpu.VMEM),
        pl.BlockSpec(memory_space=pltpu.SMEM),
        pl.BlockSpec(memory_space=pl.ANY),
    )
    dma = pltpu.SemaphoreType.DMA
    d_inputs, d_units, grads = pl.pallas_call(
        functools.partial(step_kernel, ny, nz, nb, pcol),
        out_shape=(
            jax.ShapeDtypeStruct(inputs.shape, BF),
            jax.ShapeDtypeStruct((EXP, UR, 128), F32),
            jax.ShapeDtypeStruct((8, 128), F32),
        ),
        in_specs=[hbm, hbm, vmem, smem, smem, smem, vmem],
        out_specs=(hbm, hbm, vmem),
        scratch_shapes=[
            pltpu.VMEM((nb, CG, width), BF),
            pltpu.VMEM((nb, CG, width), BF),
            pltpu.VMEM((patches, 12 * CG, PIX), BF),
            pltpu.VMEM((nz, EXP, UR, 128), BF),
            pltpu.VMEM((ny - 1, nz, UR, 128), BF),
            pltpu.VMEM((ny, nz, UR, 128), BF),
            pltpu.VMEM((patches, UR, 128), F32),
            pltpu.VMEM((ny - 1, nz, UR, 128), BF),
            pltpu.VMEM((ny, nz, UR, 128), BF),
            pltpu.VMEM((2, half, NSUB, ES, UR, 128), BF),
            pltpu.VMEM((2, half, NSUB, ES, UR, 128), BF),
            pltpu.VMEM((nb, CG, width), BF),
            pltpu.VMEM((128, 128), F32),
            pltpu.VMEM((8, 128), F32),
            pltpu.VMEM((nb, 8, 128), F32),
            pltpu.VMEM((EXP, UR, 128), F32),
            pltpu.VMEM((TAPS, 8, PIX), F32),
            pltpu.VMEM((CG, 128), F32),
            pltpu.VMEM((CG, 128), BF),
            pltpu.VMEM((EXP, UR, 128), BF),
            dma((2, nb)), dma((2, nb)), dma((2,)),
            dma((2, half, NSUB)), dma((2, half, NSUB)),
            dma((ny - 1, nz)), dma((ny - 1, nz)),
            dma((ny - 1, nz)), dma((ny - 1, nz)),
            dma((2, half, NSUB)), dma((2, half, NSUB)),
            dma((nb,)), dma((nb,)), dma((nb,)), dma((nb,)), dma((2,)),
        ],
        compiler_params=pltpu.CompilerParams(collective_id=0, has_side_effects=True),
        name="expert_step",
    )(inputs, cotangent, units, table, rows, gates, jnp.broadcast_to(gates, (8, 128)))

    main = d_units[:, :64].reshape(EXP, 2, CG, 4, CG).transpose(0, 4, 2, 1, 3).reshape(EXP, CG, CG, 8)
    last = d_units[:, 64:, :64].reshape(EXP, 16, 2, CG).transpose(0, 3, 2, 1).reshape(EXP, CG, CG, 1)
    d_weights = jnp.concatenate([main, last], axis=3).reshape(weights.shape)
    gate_grad = grads[0, :count].reshape(nb, pcol, TOP)
    return (d_inputs, d_weights, gate_grad)


def solution(mesh):
    grid_size = mesh.shape["grid"]
    nz = Z_SIZE if grid_size % Z_SIZE == 0 else grid_size // 2
    placed = (
        P("batch", None, "grid"),
        P("batch", None, "grid"),
        P("grid", "batch", None),
        P(),
        P(),
    )
    return jax.shard_map(
        functools.partial(per_device, nz),
        mesh=mesh,
        in_specs=placed,
        out_specs=(P("batch", None, "grid"), P("grid", "batch", None), P(None, "grid", None)),
        check_vma=False,
    )
```

profile of v0, /device:TPU:1, one launch (start us, length us, event | category | flops | bytes accessed | tf_op | source)
XLA Modules:
  0.0 126.0 jit_solution(4680097885910816513)
XLA Ops:
  0.7 0.7 copy-done
  1.8 0.5 pad_bitcast_fusion
  2.3 0.6 broadcast_in_dim.26.gatev_ref
  2.9 0.8 copy.64
  3.8 0.1 copy.66
  4.0 0.7 select_reduce_fusion.tab_ref
  4.7 5.6 %reshape.136 = bf16[8,32,32,9]{3,2,1,0:T(8,128)(2,1)S(1)} reshape(bf16[8,1,9216]{2,0,1:T(8,128)(2,1)} %param.7) | data formatting | bytes 294912 | tf_op jit(solution)/shard_map/reshape | solution.py:495
  10.3 1.3 %copy.60 = bf16[8,32,32,8]{2,1,3,0:T(8,128)(2,1)S(1)} copy(bf16[8,32,32,8]{3,2,1,0:T(8,128)(2,1)S(1)} %bitcast.25) | data formatting | bytes 262144 | tf_op jit(solution)/shard_map/slice | solution.py:496
  11.6 0.3 copy.61
  11.9 0.3 reshape.138
  12.2 2.0 %slice.21 = bf16[8,32,32,1]{3,2,1,0:T(8,128)(2,1)} slice(bf16[8,32,32,9]{3,2,1,0:T(8,128)(2,1)S(1)} %reshape.136), slice={[0:8], [0:32], [0:32], [8:9]} | slice | bytes 32768 | tf_op jit(solution)/shard_map/slice | solution.py:497
  14.2 3.4 %copy.62 = bf16[8,32,32,1]{1,2,0,3:T(8,128)(2,1)S(1)} copy(bf16[8,32,32,1]{3,2,1,0:T(8,128)(2,1)} %slice.21) | data formatting | bytes 32768 | tf_op jit(solution)/shard_map/slice | solution.py:497
  17.7 0.7 fusion.1.w_ref
  18.4 93.7 %expert_step.1 = (bf16[1,256,1024]{2,1,0:T(8,128)(2,1)}, f32[8,80,128]{2,1,0:T(8,128)}, f32[8,128]{1,0:T(8,128)}) custom-call(bf16[1,256,1024]{2,1,0:T(8,128)(2,1)} %x_hbm.1, bf16[1,256,1024]{2,1,0:T(8,128)(2,1)} %dy_hbm.1, bf16[8,80,128]{2,1,0:T(8,128)(2,1)} %fusion.1.w_ref, s32[4,64]{1,0:T(4,128)} %select_reduce_fusion.tab_ref, s32[4,64]{1,0:T(4,128)} %copy-done.2, ...), custom_call_target="tpu_custom_call" | custom-call | tf_op jit(solution)/shard_map/expert_step/pallas_call | solution.py:516
  112.2 0.7 slice_reduce_fusion
  113.0 0.7 copy.79
  113.7 0.8 slice.18
  114.5 1.0 slice.17
  115.7 0.4 reshape.142
  116.2 0.3 copy.74
  116.5 0.1 pad_maximum_fusion
  116.7 3.1 %copy.77 = f32[8,32,32,9]{3,2,1,0:T(8,128)} copy(f32[8,32,32,9]{2,1,3,0:T(8,128)S(1)} %pad_maximum_fusion) | data formatting | bytes 589824 | tf_op jit(solution)/shard_map/concatenate | solution.py:559
  119.7 5.5 %reshape.147 = f32[8,1,9216]{2,1,0:T(1,128)} reshape(f32[8,32,32,9]{3,2,1,0:T(8,128)} %copy.77) | data formatting | bytes 589824 | tf_op jit(solution)/shard_map/reshape | solution.py:559
  125.2 0.8 copy.83
  (20 shorter events, 1.0 us)
Async XLA Ops:
  0.6 0.7 copy-start
  4.0 7.6 %copy-start.2 = (s32[4,64]{1,0:T(4,128)}, s32[4,64]{1,0:T(4,128)S(1)}, u32[]{:S(2)}) copy-start(s32[4,64]{1,0:T(4,128)S(1)} %copy.67.rows_ref) | copy-start | bytes 3076
  119.7 5.5 %copy-start.1 = (bf16[1,256,1024]{2,1,0:T(8,128)(2,1)S(1)}, bf16[1,256,1024]{2,1,0:T(8,128)(2,1)}, u32[]{:S(2)}) copy-start(bf16[1,256,1024]{2,1,0:T(8,128)(2,1)} %get-tuple-element.31) | copy-start | bytes 1572868
where the time goes:
time: 126 us
  Pallas kernels  93.7 us (74%)
  local copies, waits for them, and re-layouts  29.9 us (24%)
  other arithmetic  1.6 us (1%)
    pallas_call x1, Pallas kernels, per_device(): pl.pallas_call(functools.partial(step_kernel, ny, nz, nb, pcol), out_shap...  93.7 us
    reshape x1, local copies, waits for them, and re-layouts, per_device(): kernels = weights.reshape(EXP, CG, CG, TAPS)  5.55 us
    reshape x1, local copies, waits for them, and re-layouts, per_device(): d_weights = jnp.concatenate([main, last], axis=3).reshape(weights.shape)  5.45 us
    slice x2, local copies, waits for them, and re-layouts, per_device(): kernels[..., 8].reshape(EXP, CG, 2, 16).transpose(0, 3, 2, 1)  5.41 us
    unnamed x10, local copies, waits for them, and re-layouts  3.12 us
    concatenate x1, local copies, waits for them, and re-layouts, per_device(): d_weights = jnp.concatenate([main, last], axis=3).reshape(weights.shape)  3.05 us

commit v1 on v0

--- a/solution.py
+++ b/solution.py
@@ -12,6 +12,7 @@
 SIDE = 16
 PIX = SIDE * SIDE
 TAPS = 9
+ROW = CG * TAPS
 EXP = 8
 TOP = 2
 NSUB = 4
@@ -24,10 +25,10 @@
 
 def step_kernel(
     ny, nz, nb, pcol,
-    x_hbm, dy_hbm, w_ref, tab_ref, rows_ref, gate_ref, gatev_ref,
+    x_hbm, dy_hbm, w_ref, tab_ref, rows_ref, logit_ref,
     dx_hbm, dw_hbm, gg_ref,
     xg, dyg, taps_buf, wg, ws, wr, gb, gs, gr, rr, rs, dxs, parts, dots_s, dots_r, dw_v,
-    tap_mask, tail_mask, tail_mask_bf, block,
+    tap_mask, tail_mask, tail_mask_bf, block, wl, flat_a, flat_t, out_v, gate_rows,
     act_send, act_recv, act_loc, ag_send, ag_recv, wy_send, wy_recv, gy_send, gy_recv,
     rs_send, rs_recv, dx_send, dx_recv, dot_send, dot_recv, out_sem,
 ):
@@ -67,6 +68,44 @@
     peers += [(grid_id, receiver_of(jnp.int32(j))) for j in range(1, nb)]
     for peer in peers:
         pl.semaphore_signal(barrier, inc=1, device_id=peer, device_id_type=MESH)
+
+    quarter = lax.div(lax.broadcasted_iota(jnp.int32, (CG, 128), 1), CG)
+    lane8 = lax.broadcasted_iota(jnp.int32, (8, 128), 1)
+    for oh in range(8):
+        flat = w_ref[:, oh * 4 * ROW : (oh + 1) * 4 * ROW].astype(F32)
+        for ol in range(4):
+            for t in range(3):
+                at = (2 * ol + t) * 128
+                piece = flat[:, at : at + 128]
+                if ol:
+                    piece = pltpu.roll(piece, 128 - CG * ol, 1)
+                    if t < 2:
+                        after = pltpu.roll(flat[:, at + 128 : at + 256], 128 - CG * ol, 1)
+                        piece = jnp.where(lane8 < 128 - CG * ol, piece, after)
+                flat_a[t, pl.ds(oh * 4 + ol, EXP, stride=CG), :] = piece
+    for h in range(2):
+        for t in range(3):
+            flat_t[h, t * 128 : (t + 1) * 128, :] = flat_a[t, h * 128 : (h + 1) * 128, :].T
+
+    def turned(value):
+        return [value] + [pltpu.roll(value, CG * k, 1) for k in range(1, 4)]
+
+    for h in range(2):
+        for th in range(2):
+            turns = [turned(flat_t[h, pl.ds(th * 4 + tl, CG, stride=TAPS), :]) for tl in range(4)]
+            for el in range(4):
+                unit = turns[0][-el % 4]
+                for tl in range(1, 4):
+                    unit = jnp.where(quarter == tl, turns[tl][(tl - el) % 4], unit)
+                wl[4 * h + el, th * CG : (th + 1) * CG, :] = unit.astype(BF)
+        turns = turned(flat_t[h, pl.ds(8, CG, stride=TAPS), :])
+        for el in range(4):
+            low, high = turns[-el % 4][:16], turns[(1 - el) % 4][16:]
+            unit = jnp.where(quarter[:16] == 0, low, jnp.where(quarter[:16] == 1, high, 0.0))
+            wl[4 * h + el, 64:80, :] = unit.astype(BF)
+
+    gates = jax.nn.sigmoid(logit_ref[...])
+    gate_rows[...] = jnp.broadcast_to(gates, (128, 128)).T
     pl.semaphore_wait(barrier, len(peers))
 
     def act_copy(which, j):
@@ -91,7 +130,7 @@
         origin = lax.rem(z + nz - (s - 1), nz) if way == 0 else lax.rem(z + (s - 1), nz)
         piece = pl.ds(c * ES, ES)
         return pltpu.make_async_remote_copy(
-            src_ref=w_ref.at[piece] if first else wg.at[origin, piece],
+            src_ref=wl.at[piece] if first else wg.at[origin, piece],
             dst_ref=wg.at[origin, piece],
             send_sem=ag_send.at[way, s - 1, c],
             recv_sem=ag_recv.at[way, s - 1, c],
@@ -153,13 +192,13 @@
 
     act_local(0).start()
     act_local(1).start()
+    for j in range(1, nb):
+        act_copy(0, jnp.int32(j)).start()
+        act_copy(1, jnp.int32(j)).start()
     for way in (0, 1):
         for c in range(NSUB):
             if half > 1 or (c < NSUB // 2) == (way == 0):
                 ag_copy(way, 1, c, True).start()
-    for j in range(1, nb):
-        act_copy(0, jnp.int32(j)).start()
-        act_copy(1, jnp.int32(j)).start()
 
     lane = lax.broadcasted_iota(jnp.int32, (8, PIX), 1)
     column = lax.rem(lane, SIDE)
@@ -220,7 +259,7 @@
         zo = lax.rem(z + rel, nz)
         for d in range(ny):
             route = lax.div(tab_ref[y, tile_at(d) * nz + zo], EXP)
-            value = (gb[lax.div(route, TOP)] * gate_ref[0, route]).astype(BF)
+            value = (gb[lax.div(route, TOP)] * gate_rows[pl.ds(route, 1), :]).astype(BF)
             if d == 0:
                 gr[0, rel] = value
             else:
@@ -251,7 +290,9 @@
             prod = (prod[0:8] + prod[8:16]) + (prod[16:24] + prod[24:32])
             prod = prod[:, :128] + prod[:, 128:]
             parts[pl.ds(index * TOP + k, 1), :] = jnp.sum(prod, axis=0, keepdims=True)
-            total = total + (gate_ref[0, index * TOP + k] * one).astype(BF).astype(F32)
+            gate = gate_rows[pl.ds(index * TOP + k, 1), :]
+            gate = jnp.concatenate([gate, gate], axis=1)
+            total = total + (gate * one).astype(BF).astype(F32)
         dxs[s, :, patch_lanes(p)] = total.astype(BF)
 
     def own_part(rel, e):
@@ -276,7 +317,7 @@
         for d in range(1, ny):
             gy_copy(d, rel).wait_recv()
 
-    wg[z] = w_ref[...]
+    wg[z] = wl[...]
     pick(jnp.int32(0))
 
     def phase_one(k, carry):
@@ -433,14 +474,48 @@
             value = own_part(jnp.int32(0), c * ES + k)
             value = value + rr[0, last, c, k].astype(F32) + rr[1, last, c, k].astype(F32)
             dw_v[c * ES + k] = value * (1.0 / SIDE)
-    out_dw = pltpu.make_async_copy(dw_v, dw_hbm, out_sem.at[1])
+    for h in range(2):
+        for th in range(2):
+            turns = [turned(dw_v[4 * h + el, th * CG : (th + 1) * CG, :]) for el in range(4)]
+            for tl in range(4):
+                value = turns[0][-tl % 4]
+                for el in range(1, 4):
+                    value = jnp.where(quarter == el, turns[el][(el - tl) % 4], value)
+                flat_t[h, pl.ds(th * 4 + tl, CG, stride=TAPS), :] = value
+        value = None
+        for el in range(4):
+            turns = turned(dw_v[4 * h + el, 64:80, :])
+            both = jnp.concatenate([turns[el], turns[(el - 1) % 4]], axis=0)
+            value = both if value is None else jnp.where(quarter == el, both, value)
+        flat_t[h, pl.ds(8, CG, stride=TAPS), :] = value
+    for h in range(2):
+        for t in range(3):
+            flat_a[t, h * 128 : (h + 1) * 128, :] = flat_t[h, t * 128 : (t + 1) * 128, :].T
+    lane64 = lax.broadcasted_iota(jnp.int32, (8 * EXP, 128), 1)
+    tiles = [None] * TAPS
+    for ol in range(4):
+        for t in range(3):
+            piece = flat_a[t, pl.ds(ol, 8 * EXP, stride=4), :]
+            if ol:
+                piece = pltpu.roll(piece, CG * ol, 1)
+            at = 2 * ol + t
+            if t == 2:
+                keep = (lane64 >= CG * ol) & (lane64 < CG * (ol + 1))
+            else:
+                keep = lane64 >= CG * ol
+            tiles[at] = jnp.where(keep, piece, 0.0 if tiles[at] is None else tiles[at])
+            if ol and t < 2:
+                at += 1
+                tiles[at] = jnp.where(lane64 < CG * ol, piece, 0.0 if tiles[at] is None else tiles[at])
+    for q in range(TAPS):
+        out_v[pl.ds(q, 8 * EXP, stride=TAPS), :] = tiles[q]
+    out_dw = pltpu.make_async_copy(out_v, dw_hbm, out_sem.at[1])
     out_dw.start()
 
     total = dots_s[...]
     for j in range(1, nb):
         dot_copy(jnp.int32(j)).wait_recv()
         total = total + dots_r[j]
-    gates = gatev_ref[...]
     gg_ref[...] = gates * (1.0 - gates) * total * (1.0 / SIDE)
 
     for j in range(1, nb):
@@ -492,11 +567,6 @@
     index = lax.axis_index("grid")
     y, z = index // nz, index % nz
 
-    kernels = weights.reshape(EXP, CG, CG, TAPS)
-    main = kernels[..., :8].reshape(EXP, CG, CG, 2, 4).transpose(0, 3, 2, 4, 1).reshape(EXP, 64, 128)
-    last = kernels[..., 8].reshape(EXP, CG, 2, 16).transpose(0, 3, 2, 1).reshape(EXP, 16, 64)
-    units = jnp.concatenate([main, jnp.pad(last, ((0, 0), (0, 0), (0, 64)))], axis=1)
-
     near = routes.reshape(nb, ny, nz, pcol, TOP)
     near = lax.dynamic_index_in_dim(near, z, 2, keepdims=False)
     rows = near.transpose(1, 0, 2, 3).reshape(ny, count)
@@ -504,8 +574,7 @@
     named = (rows // EXP)[:, None, :] == jnp.arange(grid_size, dtype=jnp.int32)[None, :, None]
     table = jnp.sum(jnp.where(named, code[:, None, :], 0), axis=2)
     own = lax.dynamic_slice_in_dim(gate_logits, index * pcol, pcol, 1).reshape(1, count)
-    gates = jax.nn.sigmoid(own)
-    gates = jnp.pad(gates, ((0, 0), (0, 128 - count)))
+    logits = jnp.pad(own, ((0, 0), (0, 128 - count)))
 
     vmem, smem, hbm = (
         pl.BlockSpec(memory_space=pltpu.VMEM),
@@ -513,14 +582,14 @@
         pl.BlockSpec(memory_space=pl.ANY),
     )
     dma = pltpu.SemaphoreType.DMA
-    d_inputs, d_units, grads = pl.pallas_call(
+    d_inputs, d_flat, grads = pl.pallas_call(
         functools.partial(step_kernel, ny, nz, nb, pcol),
         out_shape=(
             jax.ShapeDtypeStruct(inputs.shape, BF),
-            jax.ShapeDtypeStruct((EXP, UR, 128), F32),
+            jax.ShapeDtypeStruct((EXP * ROW // 4, 128), F32),
             jax.ShapeDtypeStruct((8, 128), F32),
         ),
-        in_specs=[hbm, hbm, vmem, smem, smem, smem, vmem],
+        in_specs=[hbm, hbm, vmem, smem, smem, vmem],
         out_specs=(hbm, hbm, vmem),
         scratch_shapes=[
             pltpu.VMEM((nb, CG, width), BF),
@@ -543,6 +612,11 @@
             pltpu.VMEM((CG, 128), F32),
             pltpu.VMEM((CG, 128), BF),
             pltpu.VMEM((EXP, UR, 128), BF),
+            pltpu.VMEM((EXP, UR, 128), BF),
+            pltpu.VMEM((3, EXP * CG, 128), F32),
+            pltpu.VMEM((2, 3 * 128, 128), F32),
+            pltpu.VMEM((EXP * ROW // 4, 128), F32),
+            pltpu.VMEM((128, 128), F32),
             dma((2, nb)), dma((2, nb)), dma((2,)),
             dma((2, half, NSUB)), dma((2, half, NSUB)),
             dma((ny - 1, nz)), dma((ny - 1, nz)),
@@ -552,11 +626,9 @@
         ],
         compiler_params=pltpu.CompilerParams(collective_id=0, has_side_effects=True),
         name="expert_step",
-    )(inputs, cotangent, units, table, rows, gates, jnp.broadcast_to(gates, (8, 128)))
-
-    main = d_units[:, :64].reshape(EXP, 2, CG, 4, CG).transpose(0, 4, 2, 1, 3).reshape(EXP, CG, CG, 8)
-    last = d_units[:, 64:, :64].reshape(EXP, 16, 2, CG).transpose(0, 3, 2, 1).reshape(EXP, CG, CG, 1)
-    d_weights = jnp.concatenate([main, last], axis=3).reshape(weights.shape)
+    )(inputs, cotangent, weights.reshape(EXP, CG * ROW), table, rows, logits)
+
+    d_weights = d_flat.reshape(weights.shape)
     gate_grad = grads[0, :count].reshape(nb, pcol, TOP)
     return (d_inputs, d_weights, gate_grad)
 

time: 126 us -> 102 us (0.81)
  local copies, waits for them, and re-layouts: 29.9 us -> 6.58 us
    reshape x9 -> x1, local copies, waits for them, and re-layouts: 12.4 us -> 0.11 us  [per_device(): lax.dynamic_slice_in_dim(gate_logits, index * pcol, pcol, 1)]
    slice x5 -> x0, local copies, waits for them, and re-layouts: 8.5 us -> none  [the longest x2 5.41 us: per_device(): kernels[..., 8].reshape(EXP, CG, 2, 16).transpose(0, 3, 2, 1)]
    concatenate x1 -> x0, local copies, waits for them, and re-layouts: 3.05 us -> none  [per_device(): d_weights = jnp.concatenate([main, last], axis=3).reshape(weights.shape)]
    unnamed x10 -> x12, local copies, waits for them, and re-layouts: 3.12 us -> 4.72 us
where the time goes in v1:
time: 102 us
  Pallas kernels  93.8 us (92%)
  local copies, waits for them, and re-layouts  6.58 us (6%)
    pallas_call x1, Pallas kernels, per_device(): pl.pallas_call(functools.partial(step_kernel, ny, nz, nb, pcol), out_shap...  93.8 us
    unnamed x12, local copies, waits for them, and re-layouts  4.72 us

profile of v1, /device:TPU:1, one launch (start us, length us, event | category | flops | bytes accessed | tf_op | source)
XLA Modules:
  0.0 101.8 jit_solution(4629497004866815657)
XLA Ops:
  0.6 0.0 copy-start
  0.7 0.7 copy-done
  1.4 0.1 constant_dynamic-slice_fusion
  1.4 0.0 copy-start.3
  1.4 0.1 copy.44
  1.6 0.1 reshape.90
  1.7 0.5 pad.4.logit_ref
  2.2 0.0 copy-done.3
  2.2 0.1 copy.37
  2.4 0.1 copy.39
  2.5 0.1 copy.40.rows_ref
  2.6 0.0 copy-start.2
  2.6 0.6 copy-done.2
  3.2 0.7 select_reduce_fusion.tab_ref
  3.9 93.8 %expert_step.1 = (bf16[1,256,1024]{2,1,0:T(8,128)(2,1)}, f32[576,128]{1,0:T(8,128)}, f32[8,128]{1,0:T(8,128)}) custom-call(bf16[1,256,1024]{2,1,0:T(8,128)(2,1)} %x_hbm.1, bf16[1,256,1024]{2,1,0:T(8,128)(2,1)} %dy_hbm.1, bf16[8,9216]{1,0:T(8,128)(2,1)} %bitcast.10, s32[4,64]{1,0:T(4,128)} %select_reduce_fusion.tab_ref, s32[4,64]{1,0:T(4,128)} %copy-done.2, ...), custom_call_target="tpu_custom_call" | custom-call | tf_op jit(solution)/shard_map/expert_step/pallas_call | solution.py:585
  97.7 0.7 slice_reduce_fusion
  98.4 0.1 reshape_squeeze.3
  98.5 0.7 copy.47
  99.2 0.0 copy-start.1
  99.2 1.9 %copy.51 = bf16[1,256,1024]{2,1,0:T(8,128)(2,1)} copy(bf16[1,256,1024]{2,1,0:T(8,128)(2,1)} %get-tuple-element.29) | data formatting | bytes 1048576
  101.1 0.0 copy-done.1
  101.1 0.7 copy.52
  (3 shorter events, 0.0 us)
Async XLA Ops:
  0.6 0.7 copy-start
  1.4 0.8 copy-start.3
  2.6 0.6 copy-start.2
  99.2 1.9 %copy-start.1 = (f32[576,128]{1,0:T(8,128)S(1)}, f32[576,128]{1,0:T(8,128)}, u32[]{:S(2)}) copy-start(f32[576,128]{1,0:T(8,128)} %get-tuple-element.7) | copy-start | bytes 884740

commit v2 on v1

--- a/solution.py
+++ b/solution.py
@@ -17,6 +17,7 @@
 TOP = 2
 NSUB = 4
 ES = EXP // NSUB
+PER_TICK = 2
 UR = 80
 BF = jnp.bfloat16
 F32 = jnp.float32
@@ -36,6 +37,12 @@
     nx = nb // 2
     patches = nb * pcol
     ticks = half * NSUB
+    grad_from = 1
+    stage_from = grad_from + patches // PER_TICK
+    stage_ticks = 4 if nz >= 16 else 2
+    rs_from = stage_from + stage_ticks + 1
+    dx_from = ticks + 4
+    all_ticks = rs_from + ticks
     grid_id = lax.axis_index("grid")
     b = lax.axis_index("batch")
     y = lax.div(grid_id, nz)
@@ -162,7 +169,7 @@
     def rs_copy(way, t, c):
         return pltpu.make_async_remote_copy(
             src_ref=rs.at[way, t, c],
-            dst_ref=rr.at[way, t, c],
+            dst_ref=rr.at[way, t + 1, c],
             send_sem=rs_send.at[way, t, c],
             recv_sem=rs_recv.at[way, t, c],
             device_id=(hop_to[way], b),
@@ -214,7 +221,9 @@
     tail_mask_bf[...] = tail.astype(BF)
     parts[...] = jnp.zeros_like(parts)
     for c in range(NSUB):
-        rr[1 if c < NSUB // 2 else 0, 0, c] = jnp.zeros((ES, UR, 128), BF)
+        for way in (0, 1):
+            rr[way, 0, c] = jnp.zeros((ES, UR, 128), BF)
+        rr[1 if c < NSUB // 2 else 0, 1, c] = jnp.zeros((ES, UR, 128), BF)
 
     def expert_of(tile, zo):
         return lax.rem(tab_ref[tile, y * nz + zo], EXP)
@@ -229,6 +238,9 @@
     def send_picks(rel):
         for d in range(1, ny):
             wy_copy(d, rel).start()
+
+    def route_at(s, p, k):
+        return (p * TOP + k) * nb + s
 
     def patch_lanes(p):
         return pl.ds(pl.multiple_of(p * PIX, PIX), PIX)
@@ -259,7 +271,8 @@
         zo = lax.rem(z + rel, nz)
         for d in range(ny):
             route = lax.div(tab_ref[y, tile_at(d) * nz + zo], EXP)
-            value = (gb[lax.div(route, TOP)] * gate_rows[pl.ds(route, 1), :]).astype(BF)
+            patch = lax.rem(route, nb) * pcol + lax.div(route, TOP * nb)
+            value = (gb[patch] * gate_rows[pl.ds(route, 1), :]).astype(BF)
             if d == 0:
                 gr[0, rel] = value
             else:
@@ -274,7 +287,7 @@
         index = s * pcol + p
         mains, tails = [], []
         for k in range(TOP):
-            unit = route_unit(index * TOP + k)
+            unit = route_unit(route_at(s, p, k))
             mains.append(jnp.concatenate([unit[0:32], unit[32:64]], axis=1))
             tails.append(jnp.concatenate([unit[64:80], unit[64:80]], axis=0) * tail_mask_bf[...])
         adjoint = jnp.dot(
@@ -289,8 +302,8 @@
             prod = xp * one
             prod = (prod[0:8] + prod[8:16]) + (prod[16:24] + prod[24:32])
             prod = prod[:, :128] + prod[:, 128:]
-            parts[pl.ds(index * TOP + k, 1), :] = jnp.sum(prod, axis=0, keepdims=True)
-            gate = gate_rows[pl.ds(index * TOP + k, 1), :]
+            parts[pl.ds(route_at(s, p, k), 1), :] = jnp.sum(prod, axis=0, keepdims=True)
+            gate = gate_rows[pl.ds(route_at(s, p, k), 1), :]
             gate = jnp.concatenate([gate, gate], axis=1)
             total = total + (gate * one).astype(BF).astype(F32)
         dxs[s, :, patch_lanes(p)] = total.astype(BF)
@@ -305,12 +318,10 @@
             total = term if total is None else total + term
         return total
 
-    def rs_add(way, t, c, fresh):
+    def rs_add(way, t, c):
         rel = half - t if way == 0 else nz - half + t
         for k in range(ES):
-            value = own_part(rel, c * ES + k)
-            if not fresh:
-                value = value + rr[way, t - 1, c, k].astype(F32)
+            value = own_part(rel, c * ES + k) + rr[way, t, c, k].astype(F32)
             rs[way, t, c, k] = value.astype(BF)
 
     def wait_grads(rel):
@@ -320,139 +331,182 @@
     wg[z] = wl[...]
     pick(jnp.int32(0))
 
-    def phase_one(k, carry):
+    def gather_tick(k):
         s = lax.div(k, NSUB) + 1
+        c = lax.rem(k, NSUB)
+        low = c < NSUB // 2
+
+        @pl.when(k < ticks)
+        def _():
+            for way in (0, 1):
+                mine = low if way == 0 else jnp.logical_not(low)
+
+                @pl.when(jnp.logical_or(s < half, mine))
+                def _():
+                    ag_copy(way, s, c, False).wait_recv()
+
+                @pl.when(jnp.logical_or(s + 1 < half, jnp.logical_and(s + 1 == half, mine)))
+                def _():
+                    ag_copy(way, s + 1, c, False).start()
+
+        @pl.when(jnp.logical_and(k <= ticks, c == 0))
+        def _():
+            send_picks(s - 1)
+
+            @pl.when(jnp.logical_and(s > 1, s <= half))
+            def _():
+                send_picks(nz - s + 1)
+
+        @pl.when(jnp.logical_and(k < ticks, c == NSUB - 1))
+        def _():
+            pick(s)
+
+            @pl.when(s < half)
+            def _():
+                pick(nz - s)
+
+    def grad_tick(i):
+        j = lax.div(i, pcol)
+
+        @pl.when(lax.rem(i, pcol) == 0)
+        def _():
+            @pl.when(j == 0)
+            def _():
+                act_local(0).wait()
+                act_local(1).wait()
+
+            @pl.when(j > 0)
+            def _():
+                act_copy(0, j).wait_recv()
+                act_copy(1, j).wait_recv()
+
+        def one(n, carry):
+            grad_patch(j, lax.rem(i, pcol) + n)
+            return carry
+
+        lax.fori_loop(0, PER_TICK, one, 0)
+
+    def stage_tick(k):
+        count = nz // stage_ticks
+
+        def rel_of(n):
+            i = k * count + n
+            return lax.rem(half + lax.div(i + 1, 2) * (1 - 2 * lax.rem(i, 2)) + nz, nz)
+
+        def stage(n, carry):
+            grad_stage(rel_of(n))
+            return carry
+
+        def send(n, carry):
+            for d in range(1, ny):
+                gy_copy(d, rel_of(n)).start()
+            return carry
+
+        lax.fori_loop(0, count, stage, 0)
+        lax.fori_loop(0, count, send, 0)
+
+    def scatter_start(k):
+        t = lax.div(k, NSUB)
+        c = lax.rem(k, NSUB)
+        low = c < NSUB // 2
+
+        @pl.when(c == 0)
+        def _():
+            wait_grads(half - t)
+
+            @pl.when(t > 0)
+            def _():
+                wait_grads(nz - half + t)
+
+        for way in (0, 1):
+            mine = low if way == 0 else jnp.logical_not(low)
+
+            @pl.when(jnp.logical_or(t > 1, jnp.logical_and(t == 1, mine)))
+            def _():
+                rs_copy(way, t - 1, c).wait_recv()
+
+            rs_add(way, t, c)
+
+    def scatter_send(k):
+        t = lax.div(k, NSUB)
         c = lax.rem(k, NSUB)
         low = c < NSUB // 2
         for way in (0, 1):
             mine = low if way == 0 else jnp.logical_not(low)
 
-            @pl.when(jnp.logical_or(s < half, mine))
-            def _():
-                ag_copy(way, s, c, False).wait_recv()
-
-            @pl.when(jnp.logical_or(s + 1 < half, jnp.logical_and(s + 1 == half, mine)))
-            def _():
-                ag_copy(way, s + 1, c, False).start()
-
-        @pl.when(c == 0)
-        def _():
-            send_picks(s - 1)
-
-            @pl.when(s > 1)
-            def _():
-                send_picks(nz - s + 1)
-
-        @pl.when(k < patches)
-        def _():
-            j = lax.div(k, pcol)
-
-            @pl.when(lax.rem(k, pcol) == 0)
-            def _():
-                @pl.when(j == 0)
-                def _():
-                    act_local(0).wait()
-                    act_local(1).wait()
-
-                @pl.when(j > 0)
-                def _():
-                    act_copy(0, j).wait_recv()
-                    act_copy(1, j).wait_recv()
-
-            grad_patch(j, lax.rem(k, pcol))
-
-        @pl.when(c == NSUB - 1)
-        def _():
-            pick(s)
-
-            @pl.when(s < half)
-            def _():
-                pick(nz - s)
-
-        return carry
-
-    lax.fori_loop(0, ticks, phase_one, 0)
-
-    def stage_one(i, carry):
-        rel = lax.rem(half + lax.div(i + 1, 2) * (1 - 2 * lax.rem(i, 2)) + nz, nz)
-        grad_stage(rel)
-        return carry
-
-    def stage_two(i, carry):
-        rel = lax.rem(half + lax.div(i + 1, 2) * (1 - 2 * lax.rem(i, 2)) + nz, nz)
-        for d in range(1, ny):
-            gy_copy(d, rel).start()
-        return carry
-
-    send_picks(jnp.int32(half))
-    lax.fori_loop(0, nz, stage_one, 0)
-    lax.fori_loop(0, nz, stage_two, 0)
+            @pl.when(jnp.logical_or(t > 0, mine))
+            def _():
+                rs_copy(way, t, c).start()
+
+    def dx_spot(i):
+        return nb - 1 - lax.div(i, pcol), lax.rem(i, pcol)
+
+    def dx_flush(i):
+        j, p = dx_spot(i - PER_TICK)
+
+        @pl.when(jnp.logical_and(p == pcol - PER_TICK, j > 0))
+        def _():
+            dx_copy(j).start()
 
     def wait_kernels(rel, carry):
         for d in range(1, ny):
             wy_copy(d, rel).wait_recv()
         return carry
 
+    def phase_grad(k, carry):
+        gather_tick(k)
+
+        @pl.when(k >= grad_from)
+        def _():
+            grad_tick((k - grad_from) * PER_TICK)
+
+        return carry
+
+    def phase_stage(k, carry):
+        gather_tick(k)
+
+        @pl.when(k < stage_from + stage_ticks)
+        def _():
+            stage_tick(k - stage_from)
+
+        return carry
+
+    def phase_both(k, carry):
+        gather_tick(k)
+        scatter_start(k - rs_from)
+        scatter_send(k - rs_from)
+        return carry
+
+    def phase_dx(k, carry):
+        scatter_start(k - rs_from)
+        first = (k - dx_from) * PER_TICK
+
+        def one(n, carry):
+            j, p = dx_spot(first)
+            dx_patch(j, p + n)
+            return carry
+
+        @pl.when(first < patches)
+        def _():
+            one(0, 0)
+
+        scatter_send(k - rs_from)
+
+        @pl.when(jnp.logical_and(first > 0, first <= patches))
+        def _():
+            dx_flush(first)
+
+        @pl.when(first < patches)
+        def _():
+            lax.fori_loop(1, PER_TICK, one, 0)
+
+        return carry
+
+    lax.fori_loop(0, stage_from, phase_grad, 0)
+    lax.fori_loop(stage_from, rs_from, phase_stage, 0)
+    lax.fori_loop(rs_from, dx_from, phase_both, 0)
     lax.fori_loop(0, nz, wait_kernels, 0)
-
-    wait_grads(jnp.int32(half))
-    for c in range(NSUB):
-        rs_add(0 if c < NSUB // 2 else 1, 0, c, True)
-
-    def dx_tick(k):
-        i = k - 1
-        j = nb - 1 - lax.div(i, pcol)
-
-        @pl.when(jnp.logical_and(i >= 0, i < patches))
-        def _():
-            dx_patch(j, lax.rem(i, pcol))
-
-        return i
-
-    def dx_flush(k):
-        done = k - 2
-
-        @pl.when(jnp.logical_and(done >= 0, jnp.logical_and(done < patches, lax.rem(done, pcol) == pcol - 1)))
-        def _():
-            j = nb - 1 - lax.div(done, pcol)
-
-            @pl.when(j > 0)
-            def _():
-                dx_copy(j).start()
-
-    dx_tick(jnp.int32(1))
-    for c in range(NSUB):
-        rs_copy(0 if c < NSUB // 2 else 1, 0, c).start()
-
-    def phase_two(k, carry):
-        t = lax.div(k, NSUB)
-        c = lax.rem(k, NSUB)
-        low = c < NSUB // 2
-
-        @pl.when(c == 0)
-        def _():
-            wait_grads(half - t)
-            wait_grads(nz - half + t)
-
-        for way in (0, 1):
-            mine = low if way == 0 else jnp.logical_not(low)
-
-            @pl.when(jnp.logical_or(t > 1, mine))
-            def _():
-                rs_copy(way, t - 1, c).wait_recv()
-
-            rs_add(way, t, c, False)
-        dx_flush(k - NSUB + 2)
-        dx_tick(k - NSUB + 2)
-        for way in (0, 1):
-            rs_copy(way, t, c).start()
-        return carry
-
-    lax.fori_loop(NSUB, ticks, phase_two, 0)
-    tail_ticks = range(ticks - NSUB + 2, patches + 3)
-    for k in tail_ticks:
-        dx_flush(jnp.int32(k))
-        dx_tick(jnp.int32(k))
+    lax.fori_loop(dx_from, all_ticks, phase_dx, 0)
 
     own_dx = pltpu.make_async_copy(
         dxs.at[b], dx_hbm.at[0, pl.ds(pl.multiple_of(b * CG, CG), CG), :], out_sem.at[0]
@@ -472,8 +526,7 @@
                 dot_copy(jnp.int32(j)).start()
         for k in range(ES):
             value = own_part(jnp.int32(0), c * ES + k)
-            value = value + rr[0, last, c, k].astype(F32) + rr[1, last, c, k].astype(F32)
-            dw_v[c * ES + k] = value * (1.0 / SIDE)
+            dw_v[c * ES + k] = value + rr[0, half, c, k].astype(F32) + rr[1, half, c, k].astype(F32)
     for h in range(2):
         for th in range(2):
             turns = [turned(dw_v[4 * h + el, th * CG : (th + 1) * CG, :]) for el in range(4)]
@@ -516,7 +569,12 @@
     for j in range(1, nb):
         dot_copy(jnp.int32(j)).wait_recv()
         total = total + dots_r[j]
-    gg_ref[...] = gates * (1.0 - gates) * total * (1.0 / SIDE)
+    total = gates * (1.0 - gates) * total[:1] * (1.0 / SIDE)
+    for p in range(pcol):
+        for k in range(TOP):
+            spot = (p * TOP + k) * nb
+            turn = total if spot == 0 else pltpu.roll(total, 128 - spot, 1)
+            gg_ref[p, k : k + 1, :] = turn[:, :nb]
 
     for j in range(1, nb):
         act_copy(0, jnp.int32(j)).wait_send()
@@ -569,11 +627,11 @@
 
     near = routes.reshape(nb, ny, nz, pcol, TOP)
     near = lax.dynamic_index_in_dim(near, z, 2, keepdims=False)
-    rows = near.transpose(1, 0, 2, 3).reshape(ny, count)
+    rows = near.transpose(1, 2, 3, 0).reshape(ny, count)
     code = jnp.arange(count, dtype=jnp.int32)[None, :] * EXP + rows % EXP
     named = (rows // EXP)[:, None, :] == jnp.arange(grid_size, dtype=jnp.int32)[None, :, None]
     table = jnp.sum(jnp.where(named, code[:, None, :], 0), axis=2)
-    own = lax.dynamic_slice_in_dim(gate_logits, index * pcol, pcol, 1).reshape(1, count)
+    own = lax.dynamic_slice_in_dim(gate_logits, index * pcol, pcol, 1).transpose(1, 2, 0).reshape(1, count)
     logits = jnp.pad(own, ((0, 0), (0, 128 - count)))
 
     vmem, smem, hbm = (
@@ -587,7 +645,7 @@
         out_shape=(
             jax.ShapeDtypeStruct(inputs.shape, BF),
             jax.ShapeDtypeStruct((EXP * ROW // 4, 128), F32),
-            jax.ShapeDtypeStruct((8, 128), F32),
+            jax.ShapeDtypeStruct((pcol, TOP, nb), F32),
         ),
         in_specs=[hbm, hbm, vmem, smem, smem, vmem],
         out_specs=(hbm, hbm, vmem),
@@ -601,7 +659,7 @@
             pltpu.VMEM((patches, UR, 128), F32),
             pltpu.VMEM((ny - 1, nz, UR, 128), BF),
             pltpu.VMEM((ny, nz, UR, 128), BF),
-            pltpu.VMEM((2, half, NSUB, ES, UR, 128), BF),
+            pltpu.VMEM((2, half + 1, NSUB, ES, UR, 128), BF),
             pltpu.VMEM((2, half, NSUB, ES, UR, 128), BF),
             pltpu.VMEM((nb, CG, width), BF),
             pltpu.VMEM((128, 128), F32),
@@ -628,8 +686,8 @@
         name="expert_step",
     )(inputs, cotangent, weights.reshape(EXP, CG * ROW), table, rows, logits)
 
-    d_weights = d_flat.reshape(weights.shape)
-    gate_grad = grads[0, :count].reshape(nb, pcol, TOP)
+    d_weights = (d_flat * (1.0 / SIDE)).reshape(weights.shape)
+    gate_grad = grads.transpose(2, 0, 1)
     return (d_inputs, d_weights, gate_grad)
 
 

time: 102 us -> 90.3 us (0.89)
  Pallas kernels: 93.8 us -> 83.1 us
  local copies, waits for them, and re-layouts: 6.58 us -> 3.67 us
  other arithmetic: 0.75 us -> 2.5 us
    pallas_call x1, Pallas kernels: 93.8 us -> 83.1 us  [per_device(): pl.pallas_call(functools.partial(step_kernel, ny, nz, nb, pcol), out_shap...]
    unnamed x12 -> x13, local copies, waits for them, and re-layouts: 4.72 us -> 2.78 us
    mul x0 -> x1, other arithmetic: none -> 1.75 us  [per_device(): d_weights = (d_flat * (1.0 / SIDE)).reshape(weights.shape)]
where the time goes in v2:
time: 90.3 us; the launch traced here: 90 us
  Pallas kernels  83.1 us (92%)
  local copies, waits for them, and re-layouts  3.67 us (4%)
  other arithmetic  2.5 us (3%)
    pallas_call x1, Pallas kernels, per_device(): pl.pallas_call(functools.partial(step_kernel, ny, nz, nb, pcol), out_shap...  83.1 us
    unnamed x13, local copies, waits for them, and re-layouts  2.78 us

profile of v2, /device:TPU:1, one launch (start us, length us, event | category | flops | bytes accessed | tf_op | source)
XLA Modules:
  0.0 90.0 jit_solution(5231317879503433769)
XLA Ops:
  0.6 0.0 copy-start
  0.7 0.7 copy-done
  1.4 0.0 copy-start.3
  1.4 0.1 dynamic-slice_bitcast_fusion.1
  1.4 0.1 copy.22
  1.5 0.1 reshape.90
  1.6 0.5 pad.4.logit_ref
  2.1 0.0 copy-done.3
  2.1 0.1 copy.19
  2.3 0.1 reshape.89.rows_ref
  2.4 0.0 copy-start.2
  2.4 0.6 copy-done.2
  3.0 0.7 select_reduce_fusion.tab_ref
  3.7 83.1 %expert_step.1 = (bf16[1,256,1024]{2,1,0:T(8,128)(2,1)}, f32[576,128]{1,0:T(8,128)}, f32[4,2,8]{2,1,0:T(2,128)}) custom-call(bf16[1,256,1024]{2,1,0:T(8,128)(2,1)} %x_hbm.1, bf16[1,256,1024]{2,1,0:T(8,128)(2,1)} %dy_hbm.1, bf16[8,9216]{1,0:T(8,128)(2,1)} %bitcast.12, s32[4,64]{1,0:T(4,128)} %select_reduce_fusion.tab_ref, s32[4,64]{1,0:T(4,128)} %copy-done.2, ...), custom_call_target="tpu_custom_call" | custom-call | tf_op jit(solution)/shard_map/expert_step/pallas_call | solution.py:643
  86.8 0.0 copy-start.1
  86.9 1.8 %broadcast_multiply_fusion = f32[576,128]{1,0:T(8,128)} fusion(f32[576,128]{1,0:T(8,128)} %get-tuple-element.7), kind=kLoop, calls=%fused_computation | loop fusion | flops 73728 | bytes 589824 | tf_op jit(solution)/shard_map/mul | solution.py:689
  88.6 0.0 copy-done.1
  88.6 0.0 copy-start.4
  88.6 0.8 copy.27
  89.4 0.0 copy-done.4
  89.4 0.6 copy.28
  (4 shorter events, 0.0 us)
Async XLA Ops:
  0.6 0.7 copy-start
  1.4 0.8 copy-start.3
  2.4 0.6 copy-start.2
  86.8 1.8 %copy-start.1 = (bf16[1,256,1024]{2,1,0:T(8,128)(2,1)S(1)}, bf16[1,256,1024]{2,1,0:T(8,128)(2,1)}, u32[]{:S(2)}) copy-start(bf16[1,256,1024]{2,1,0:T(8,128)(2,1)} %get-tuple-element.26) | copy-start | bytes 1572868
  88.6 0.8 copy-start.4

commit v3 on v2

--- a/solution.py
+++ b/solution.py
@@ -17,8 +17,10 @@
 TOP = 2
 NSUB = 4
 ES = EXP // NSUB
-PER_TICK = 2
+DX_GAP = 4
 UR = 80
+MR = 64
+PR = ES * MR + 16
 BF = jnp.bfloat16
 F32 = jnp.float32
 Z_SIZE = 16
@@ -37,12 +39,13 @@
     nx = nb // 2
     patches = nb * pcol
     ticks = half * NSUB
-    grad_from = 1
-    stage_from = grad_from + patches // PER_TICK
+    stage_from = nb
     stage_ticks = 4 if nz >= 16 else 2
     rs_from = stage_from + stage_ticks + 1
-    dx_from = ticks + 4
-    all_ticks = rs_from + ticks
+    pick_from = ticks - 2 * half
+    dx_from = ticks + DX_GAP
+    rs_end = rs_from + ticks
+    all_ticks = max(rs_end, dx_from + nb)
     grid_id = lax.axis_index("grid")
     b = lax.axis_index("batch")
     y = lax.div(grid_id, nz)
@@ -104,12 +107,15 @@
                 unit = turns[0][-el % 4]
                 for tl in range(1, 4):
                     unit = jnp.where(quarter == tl, turns[tl][(tl - el) % 4], unit)
-                wl[4 * h + el, th * CG : (th + 1) * CG, :] = unit.astype(BF)
+                at = el % 2 * MR + th * CG
+                wl[2 * h + el // 2, at : at + CG, :] = unit.astype(BF)
         turns = turned(flat_t[h, pl.ds(8, CG, stride=TAPS), :])
-        for el in range(4):
-            low, high = turns[-el % 4][:16], turns[(1 - el) % 4][16:]
-            unit = jnp.where(quarter[:16] == 0, low, jnp.where(quarter[:16] == 1, high, 0.0))
-            wl[4 * h + el, 64:80, :] = unit.astype(BF)
+        for pair in range(2):
+            unit = jnp.zeros((16, 128), F32)
+            for spot in range(4):
+                el, ih = 2 * pair + spot // 2, spot % 2
+                unit = jnp.where(quarter[:16] == spot, turns[(spot - el) % 4][16 * ih : 16 * ih + 16], unit)
+            wl[2 * h + pair, ES * MR :, :] = unit.astype(BF)
 
     gates = jax.nn.sigmoid(logit_ref[...])
     gate_rows[...] = jnp.broadcast_to(gates, (128, 128)).T
@@ -135,10 +141,9 @@
 
     def ag_copy(way, s, c, first):
         origin = lax.rem(z + nz - (s - 1), nz) if way == 0 else lax.rem(z + (s - 1), nz)
-        piece = pl.ds(c * ES, ES)
         return pltpu.make_async_remote_copy(
-            src_ref=wl.at[piece] if first else wg.at[origin, piece],
-            dst_ref=wg.at[origin, piece],
+            src_ref=wl.at[c] if first else wg.at[origin, c],
+            dst_ref=wg.at[origin, c],
             send_sem=ag_send.at[way, s - 1, c],
             recv_sem=ag_recv.at[way, s - 1, c],
             device_id=(hop_to[way], b),
@@ -216,21 +221,25 @@
         tap_mask[t] = jnp.where(inside, 1.0, 0.0).astype(F32)
     tail_row = lax.div(lax.broadcasted_iota(jnp.int32, (CG, 128), 0), 16)
     tail_lane = lax.div(lax.broadcasted_iota(jnp.int32, (CG, 128), 1), CG)
-    tail = jnp.where(tail_row == tail_lane, 1.0, 0.0).astype(F32)
-    tail_mask[...] = tail
-    tail_mask_bf[...] = tail.astype(BF)
+    tail_mask[...] = jnp.where(lax.rem(tail_lane, 2) == tail_row, 1.0, 0.0).astype(F32)
+    for k in range(2):
+        tail_mask_bf[k] = jnp.where(tail_lane == 2 * k + tail_row, 1.0, 0.0).astype(F32).astype(BF)
+    first_half = lax.broadcasted_iota(jnp.int32, (16, 128), 1) < 64
     parts[...] = jnp.zeros_like(parts)
     for c in range(NSUB):
         for way in (0, 1):
-            rr[way, 0, c] = jnp.zeros((ES, UR, 128), BF)
-        rr[1 if c < NSUB // 2 else 0, 1, c] = jnp.zeros((ES, UR, 128), BF)
+            rr[way, 0, c] = jnp.zeros((PR, 128), BF)
+        rr[1 if c < NSUB // 2 else 0, 1, c] = jnp.zeros((PR, 128), BF)
 
     def expert_of(tile, zo):
         return lax.rem(tab_ref[tile, y * nz + zo], EXP)
 
     def pick(rel):
         zo = lax.rem(z + rel, nz)
-        block[...] = wg[zo]
+        for e in range(EXP):
+            at = e % 2 * MR
+            block[e, :MR] = wg[zo, e // 2, at : at + MR, :]
+            block[e, MR:] = wg[zo, e // 2, ES * MR :, :]
         wr[y, zo] = block[expert_of(y, zo)]
         for d in range(1, ny):
             ws[d - 1, rel] = block[expert_of(tile_at(d), zo)]
@@ -279,17 +288,18 @@
                 gs[d - 1, rel] = value
 
     def route_unit(route):
-        owner = lax.div(rows_ref[y, route], EXP)
-        return wr[lax.div(owner, nz), lax.rem(owner, nz)]
+        expert = rows_ref[y, route]
+        owner = lax.div(expert, EXP)
+        return wr[lax.div(owner, nz), lax.rem(owner, nz)], tail_mask_bf[lax.rem(expert, 2)]
 
     def dx_patch(j, p):
         s = sender_of(j)
         index = s * pcol + p
         mains, tails = [], []
         for k in range(TOP):
-            unit = route_unit(route_at(s, p, k))
+            unit, mask = route_unit(route_at(s, p, k))
             mains.append(jnp.concatenate([unit[0:32], unit[32:64]], axis=1))
-            tails.append(jnp.concatenate([unit[64:80], unit[64:80]], axis=0) * tail_mask_bf[...])
+            tails.append(jnp.concatenate([unit[64:80], unit[64:80]], axis=0) * mask)
         adjoint = jnp.dot(
             jnp.concatenate(mains, axis=0), taps_buf[index, : 8 * CG, :], preferred_element_type=F32
         ) + jnp.dot(
@@ -308,21 +318,24 @@
             total = total + (gate * one).astype(BF).astype(F32)
         dxs[s, :, patch_lanes(p)] = total.astype(BF)
 
-    def own_part(rel, e):
+    def own_piece(rel, c):
         zo = lax.rem(z + rel, nz)
-        total = None
+        parts_of = [None] * 3
         for d in range(ny):
-            tile = lax.rem(y + ny - d, ny)
-            hit = jnp.where(expert_of(tile, zo) == e, 1.0, 0.0).astype(F32)
-            term = gr[d, rel].astype(F32) * hit
-            total = term if total is None else total + term
-        return total
+            expert = expert_of(lax.rem(y + ny - d, ny), zo)
+            hits = [jnp.where(expert == c * ES + k, 1.0, 0.0).astype(F32) for k in range(ES)]
+            main = gr[d, rel, :MR].astype(F32)
+            last = gr[d, rel, MR:].astype(F32)
+            terms = [main * hits[0], main * hits[1], last * jnp.where(first_half, hits[0], hits[1])]
+            parts_of = [b if a is None else a + b for a, b in zip(parts_of, terms)]
+        return parts_of
+
+    piece_rows = (slice(0, MR), slice(MR, ES * MR), slice(ES * MR, PR))
 
     def rs_add(way, t, c):
         rel = half - t if way == 0 else nz - half + t
-        for k in range(ES):
-            value = own_part(rel, c * ES + k) + rr[way, t, c, k].astype(F32)
-            rs[way, t, c, k] = value.astype(BF)
+        for rows, value in zip(piece_rows, own_piece(rel, c)):
+            rs[way, t, c, rows, :] = (value + rr[way, t, c, rows, :].astype(F32)).astype(BF)
 
     def wait_grads(rel):
         for d in range(1, ny):
@@ -349,13 +362,16 @@
                 def _():
                     ag_copy(way, s + 1, c, False).start()
 
-        @pl.when(jnp.logical_and(k <= ticks, c == 0))
-        def _():
-            send_picks(s - 1)
-
-            @pl.when(jnp.logical_and(s > 1, s <= half))
+        turn = k - pick_from
+        i = lax.div(turn, 2)
+
+        @pl.when(jnp.logical_and(turn >= 0, jnp.logical_and(i * 2 == turn, i <= half)))
+        def _():
+            send_picks(i)
+
+            @pl.when(jnp.logical_and(i > 0, i < half))
             def _():
-                send_picks(nz - s + 1)
+                send_picks(nz - i)
 
         @pl.when(jnp.logical_and(k < ticks, c == NSUB - 1))
         def _():
@@ -365,26 +381,22 @@
             def _():
                 pick(nz - s)
 
-    def grad_tick(i):
-        j = lax.div(i, pcol)
-
-        @pl.when(lax.rem(i, pcol) == 0)
-        def _():
-            @pl.when(j == 0)
-            def _():
-                act_local(0).wait()
-                act_local(1).wait()
-
-            @pl.when(j > 0)
-            def _():
-                act_copy(0, j).wait_recv()
-                act_copy(1, j).wait_recv()
-
-        def one(n, carry):
-            grad_patch(j, lax.rem(i, pcol) + n)
+    def grad_tick(j):
+        @pl.when(j == 0)
+        def _():
+            act_local(0).wait()
+            act_local(1).wait()
+
+        @pl.when(j > 0)
+        def _():
+            act_copy(0, j).wait_recv()
+            act_copy(1, j).wait_recv()
+
+        def one(p, carry):
+            grad_patch(j, p)
             return carry
 
-        lax.fori_loop(0, PER_TICK, one, 0)
+        lax.fori_loop(0, pcol, one, 0)
 
     def stage_tick(k):
         count = nz // stage_ticks
@@ -438,28 +450,14 @@
             def _():
                 rs_copy(way, t, c).start()
 
-    def dx_spot(i):
-        return nb - 1 - lax.div(i, pcol), lax.rem(i, pcol)
-
-    def dx_flush(i):
-        j, p = dx_spot(i - PER_TICK)
-
-        @pl.when(jnp.logical_and(p == pcol - PER_TICK, j > 0))
-        def _():
-            dx_copy(j).start()
-
     def wait_kernels(rel, carry):
         for d in range(1, ny):
             wy_copy(d, rel).wait_recv()
         return carry
 
     def phase_grad(k, carry):
+        grad_tick(k)
         gather_tick(k)
-
-        @pl.when(k >= grad_from)
-        def _():
-            grad_tick((k - grad_from) * PER_TICK)
-
         return carry
 
     def phase_stage(k, carry):
@@ -478,27 +476,31 @@
         return carry
 
     def phase_dx(k, carry):
-        scatter_start(k - rs_from)
-        first = (k - dx_from) * PER_TICK
-
-        def one(n, carry):
-            j, p = dx_spot(first)
-            dx_patch(j, p + n)
+        @pl.when(k < rs_end)
+        def _():
+            scatter_start(k - rs_from)
+
+        j = nb - 1 - (k - dx_from)
+
+        def one(p, carry):
+            dx_patch(j, p)
             return carry
 
-        @pl.when(first < patches)
+        @pl.when(j >= 0)
         def _():
             one(0, 0)
 
-        scatter_send(k - rs_from)
-
-        @pl.when(jnp.logical_and(first > 0, first <= patches))
-        def _():
-            dx_flush(first)
-
-        @pl.when(first < patches)
-        def _():
-            lax.fori_loop(1, PER_TICK, one, 0)
+        @pl.when(k < rs_end)
+        def _():
+            scatter_send(k - rs_from)
+
+        @pl.when(jnp.logical_and(j + 1 > 0, j + 1 < nb))
+        def _():
+            dx_copy(j + 1).start()
+
+        @pl.when(j >= 0)
+        def _():
+            lax.fori_loop(1, pcol, one, 0)
 
         return carry
 
@@ -507,7 +509,6 @@
     lax.fori_loop(rs_from, dx_from, phase_both, 0)
     lax.fori_loop(0, nz, wait_kernels, 0)
     lax.fori_loop(dx_from, all_ticks, phase_dx, 0)
-
     own_dx = pltpu.make_async_copy(
         dxs.at[b], dx_hbm.at[0, pl.ds(pl.multiple_of(b * CG, CG), CG), :], out_sem.at[0]
     )
@@ -524,9 +525,14 @@
         if c == 0:
             for j in range(1, nb):
                 dot_copy(jnp.int32(j)).start()
-        for k in range(ES):
-            value = own_part(jnp.int32(0), c * ES + k)
-            dw_v[c * ES + k] = value + rr[0, half, c, k].astype(F32) + rr[1, half, c, k].astype(F32)
+        value = [
+            v + rr[0, half, c, rows, :].astype(F32) + rr[1, half, c, rows, :].astype(F32)
+            for rows, v in zip(piece_rows, own_piece(jnp.int32(0), c))
+        ]
+        dw_v[ES * c, :MR] = value[0]
+        dw_v[ES * c + 1, :MR] = value[1]
+        dw_v[ES * c, MR:] = value[2]
+        dw_v[ES * c + 1, MR:] = pltpu.roll(value[2], 64, 1)
     for h in range(2):
         for th in range(2):
             turns = [turned(dw_v[4 * h + el, th * CG : (th + 1) * CG, :]) for el in range(4)]
@@ -653,14 +659,14 @@
             pltpu.VMEM((nb, CG, width), BF),
             pltpu.VMEM((nb, CG, width), BF),
             pltpu.VMEM((patches, 12 * CG, PIX), BF),
-            pltpu.VMEM((nz, EXP, UR, 128), BF),
+            pltpu.VMEM((nz, NSUB, PR, 128), BF),
             pltpu.VMEM((ny - 1, nz, UR, 128), BF),
             pltpu.VMEM((ny, nz, UR, 128), BF),
             pltpu.VMEM((patches, UR, 128), F32),
             pltpu.VMEM((ny - 1, nz, UR, 128), BF),
             pltpu.VMEM((ny, nz, UR, 128), BF),
-            pltpu.VMEM((2, half + 1, NSUB, ES, UR, 128), BF),
-            pltpu.VMEM((2, half, NSUB, ES, UR, 128), BF),
+            pltpu.VMEM((2, half + 1, NSUB, PR, 128), BF),
+            pltpu.VMEM((2, half, NSUB, PR, 128), BF),
             pltpu.VMEM((nb, CG, width), BF),
             pltpu.VMEM((128, 128), F32),
             pltpu.VMEM((8, 128), F32),
@@ -668,9 +674,9 @@
             pltpu.VMEM((EXP, UR, 128), F32),
             pltpu.VMEM((TAPS, 8, PIX), F32),
             pltpu.VMEM((CG, 128), F32),
-            pltpu.VMEM((CG, 128), BF),
+            pltpu.VMEM((2, CG, 128), BF),
             pltpu.VMEM((EXP, UR, 128), BF),
-            pltpu.VMEM((EXP, UR, 128), BF),
+            pltpu.VMEM((NSUB, PR, 128), BF),
             pltpu.VMEM((3, EXP * CG, 128), F32),
             pltpu.VMEM((2, 3 * 128, 128), F32),
             pltpu.VMEM((EXP * ROW // 4, 128), F32),

time: 90.3 us -> 88.2 us (0.977)
  Pallas kernels: 83.1 us -> 81 us
    pallas_call x1, Pallas kernels: 83.1 us -> 81 us  [per_device(): pl.pallas_call(functools.partial(step_kernel, ny, nz, nb, pcol), out_shap...]
where the time goes in v3:
time: 88.2 us; the launch traced here: 87.9 us
  Pallas kernels  81 us (92%)
  local copies, waits for them, and re-layouts  3.67 us (4%)
  other arithmetic  2.5 us (3%)
    pallas_call x1, Pallas kernels, per_device(): pl.pallas_call(functools.partial(step_kernel, ny, nz, nb, pcol), out_shap...  81 us
    unnamed x13, local copies, waits for them, and re-layouts  2.78 us

profile of v3, /device:TPU:1, one launch (start us, length us, event | category | flops | bytes accessed | tf_op | source)
XLA Modules:
  0.0 87.9 jit_solution(2709511265300067299)
XLA Ops:
  0.6 0.0 copy-start
  0.7 0.7 copy-done
  1.4 0.0 copy-start.3
  1.4 0.1 dynamic-slice_bitcast_fusion.1
  1.4 0.1 copy.22
  1.5 0.1 reshape.90
  1.6 0.5 pad.4.logit_ref
  2.1 0.0 copy-done.3
  2.1 0.1 copy.19
  2.3 0.1 reshape.89.rows_ref
  2.4 0.0 copy-start.2
  2.4 0.6 copy-done.2
  3.0 0.7 select_reduce_fusion.tab_ref
  3.7 81.0 %expert_step.1 = (bf16[1,256,1024]{2,1,0:T(8,128)(2,1)}, f32[576,128]{1,0:T(8,128)}, f32[4,2,8]{2,1,0:T(2,128)}) custom-call(bf16[1,256,1024]{2,1,0:T(8,128)(2,1)} %x_hbm.1, bf16[1,256,1024]{2,1,0:T(8,128)(2,1)} %dy_hbm.1, bf16[8,9216]{1,0:T(8,128)(2,1)} %bitcast.12, s32[4,64]{1,0:T(4,128)} %select_reduce_fusion.tab_ref, s32[4,64]{1,0:T(4,128)} %copy-done.2, ...), custom_call_target="tpu_custom_call" | custom-call | tf_op jit(solution)/shard_map/expert_step/pallas_call | solution.py:649
  84.8 0.0 copy-start.1
  84.8 1.8 %broadcast_multiply_fusion = f32[576,128]{1,0:T(8,128)} fusion(f32[576,128]{1,0:T(8,128)} %get-tuple-element.7), kind=kLoop, calls=%fused_computation | loop fusion | flops 73728 | bytes 589824 | tf_op jit(solution)/shard_map/mul | solution.py:695
  86.5 0.0 copy-done.1
  86.5 0.0 copy-start.4
  86.5 0.8 copy.27
  87.3 0.0 copy-done.4
  87.3 0.6 copy.28
  (4 shorter events, 0.0 us)
Async XLA Ops:
  0.6 0.7 copy-start
  1.4 0.8 copy-start.3
  2.4 0.6 copy-start.2
  84.8 1.8 %copy-start.1 = (bf16[1,256,1024]{2,1,0:T(8,128)(2,1)S(1)}, bf16[1,256,1024]{2,1,0:T(8,128)(2,1)}, u32[]{:S(2)}) copy-start(bf16[1,256,1024]{2,1,0:T(8,128)(2,1)} %get-tuple-element.26) | copy-start | bytes 1572868
  86.5 0.8 copy-start.4

commit v4 on v3

--- a/solution.py
+++ b/solution.py
@@ -332,9 +332,8 @@
 
     piece_rows = (slice(0, MR), slice(MR, ES * MR), slice(ES * MR, PR))
 
-    def rs_add(way, t, c):
-        rel = half - t if way == 0 else nz - half + t
-        for rows, value in zip(piece_rows, own_piece(rel, c)):
+    def rs_add(way, t, c, own):
+        for rows, value in zip(piece_rows, own):
             rs[way, t, c, rows, :] = (value + rr[way, t, c, rows, :].astype(F32)).astype(BF)
 
     def wait_grads(rel):
@@ -430,6 +429,7 @@
             def _():
                 wait_grads(nz - half + t)
 
+        own = (own_piece(half - t, c), own_piece(nz - half + t, c))
         for way in (0, 1):
             mine = low if way == 0 else jnp.logical_not(low)
 
@@ -437,7 +437,7 @@
             def _():
                 rs_copy(way, t - 1, c).wait_recv()
 
-            rs_add(way, t, c)
+            rs_add(way, t, c, own[way])
 
     def scatter_send(k):
         t = lax.div(k, NSUB)

time: 88.2 us -> 88.1 us (level)
  no operation moved by 1% of the time
where the time goes in v4:
time: 88.1 us; the launch traced here: 87.8 us
  Pallas kernels  80.9 us (92%)
  local copies, waits for them, and re-layouts  3.67 us (4%)
  other arithmetic  2.5 us (3%)
    pallas_call x1, Pallas kernels, per_device(): pl.pallas_call(functools.partial(step_kernel, ny, nz, nb, pcol), out_shap...  80.9 us
    unnamed x13, local copies, waits for them, and re-layouts  2.78 us

profile of v4, /device:TPU:1, one launch (start us, length us, event | category | flops | bytes accessed | tf_op | source)
XLA Modules:
  0.0 87.8 jit_solution(7045195222808856500)
XLA Ops:
  0.6 0.0 copy-start
  0.7 0.7 copy-done
  1.4 0.0 copy-start.3
  1.4 0.1 dynamic-slice_bitcast_fusion.1
  1.4 0.1 copy.22
  1.5 0.1 reshape.90
  1.6 0.5 pad.4.logit_ref
  2.1 0.0 copy-done.3
  2.1 0.1 copy.19
  2.3 0.1 reshape.89.rows_ref
  2.4 0.0 copy-start.2
  2.4 0.6 copy-done.2
  3.0 0.7 select_reduce_fusion.tab_ref
  3.7 80.9 %expert_step.1 = (bf16[1,256,1024]{2,1,0:T(8,128)(2,1)}, f32[576,128]{1,0:T(8,128)}, f32[4,2,8]{2,1,0:T(2,128)}) custom-call(bf16[1,256,1024]{2,1,0:T(8,128)(2,1)} %x_hbm.1, bf16[1,256,1024]{2,1,0:T(8,128)(2,1)} %dy_hbm.1, bf16[8,9216]{1,0:T(8,128)(2,1)} %bitcast.12, s32[4,64]{1,0:T(4,128)} %select_reduce_fusion.tab_ref, s32[4,64]{1,0:T(4,128)} %copy-done.2, ...), custom_call_target="tpu_custom_call" | custom-call | tf_op jit(solution)/shard_map/expert_step/pallas_call | solution.py:649
  84.6 0.0 copy-start.1
  84.7 1.8 %broadcast_multiply_fusion = f32[576,128]{1,0:T(8,128)} fusion(f32[576,128]{1,0:T(8,128)} %get-tuple-element.7), kind=kLoop, calls=%fused_computation | loop fusion | flops 73728 | bytes 589824 | tf_op jit(solution)/shard_map/mul | solution.py:695
  86.4 0.0 copy-done.1
  86.4 0.0 copy-start.4
  86.4 0.8 copy.27
  87.2 0.0 copy-done.4
  87.2 0.6 copy.28
  (4 shorter events, 0.0 us)
Async XLA Ops:
  0.6 0.7 copy-start
  1.4 0.8 copy-start.3
  2.4 0.6 copy-start.2
  84.6 1.8 %copy-start.1 = (bf16[1,256,1024]{2,1,0:T(8,128)(2,1)S(1)}, bf16[1,256,1024]{2,1,0:T(8,128)(2,1)}, u32[]{:S(2)}) copy-start(bf16[1,256,1024]{2,1,0:T(8,128)(2,1)} %get-tuple-element.26) | copy-start | bytes 1572868
  86.4 0.8 copy-start.4
